TPU v7x, 1024 devices: a whole 4x8x16 slice. The times are simulated.
1024 devices in a mesh: seq: 32 (over y, z_hi, core), chan: 32 (over x, z_lo).
Axes of the slice: x: 4, y: 8, z: 16 (z_hi: 2, z_lo: 8; z = z_hi * 8 + z_lo), core: 2. Of those that a mesh axis runs over, the one named last changes fastest.
Arguments:
- query_rows: bfloat16 [4096, 8192], P('seq', 'chan'), may hold values from -6 to 6
- key_rows: bfloat16 [4096, 8192], P('seq', 'chan'), may hold values from -6 to 6
- value_rows: bfloat16 [4096, 8192], P('seq', 'chan'), may hold values from -6 to 6
- short_taps: float32 [3, 3, 8192], P(None, None, 'chan'), may hold values from -3.5 to 3.5
- long_filter: float32 [4096, 128], P('seq'), may hold values from -1.1 to 1.1
- cotangent: bfloat16 [4096, 8192], P('seq', 'chan'), may hold values from -6 to 6
Outputs:
- hyena_out: bfloat16 [4096, 8192], P('seq', 'chan')
- grad_query: bfloat16 [4096, 8192], P('seq', 'chan')
- grad_key: bfloat16 [4096, 8192], P('seq', 'chan')
- grad_value: bfloat16 [4096, 8192], P('seq', 'chan')
- grad_filter: float32 [4096, 128], P('seq')
All inputs are finite; a program needn't handle non-finite values.
Results may differ from a plain program's by a relative error of at most 0.001.
Values may be sent and summed in bfloat16 or wider, within the bound.
A program may use at most 32 MiB of HBM per device.

v0:
```python
import math

import jax
import jax.numpy as jnp
from jax import lax
from jax.sharding import PartitionSpec as P


def shifted(block, axis, distance):
    devices = range(lax.axis_size(axis))
    route = [(i - distance, i) for i in devices if i - distance in devices]
    return lax.ppermute(block, axis, route)


def product(matrix, operand, pattern):
    return jnp.einsum(pattern, matrix, operand, precision=lax.Precision.HIGHEST)


def phase_table(outer_size, inner_size, period, offset):
    column = lax.iota(jnp.int32, outer_size)[:, None]
    row_index = offset + lax.iota(jnp.int32, inner_size)[None, :]
    turn_count = column * row_index % period
    phase_angle = turn_count.astype(jnp.float32) * (2.0 * math.pi / period)
    return (jnp.cos(phase_angle), jnp.sin(phase_angle))


def forward_first(values, offset, period):
    blocks = values.shape[0]
    slab_rows = values.shape[1]
    cosine_table, sine_table = phase_table(2 * blocks, blocks, 2 * blocks, 0)
    real_part = product(cosine_table, values, "kn,njw->kjw")
    imag_part = -product(sine_table, values, "kn,njw->kjw")
    twist_cos, twist_sin = phase_table(2 * blocks, slab_rows, period, offset)
    twist_cos = twist_cos[:, :, None]
    twist_sin = twist_sin[:, :, None]
    return jnp.stack(
        [
            real_part * twist_cos + imag_part * twist_sin,
            imag_part * twist_cos - real_part * twist_sin,
        ],
        axis=2,
    )


def forward_second(mixed_in):
    length = mixed_in.shape[1]
    cosine_table, sine_table = phase_table(length, length, length, 0)
    real_in = mixed_in[:, :, 0]
    imag_in = mixed_in[:, :, 1]
    pattern = "mn,anw->amw"
    real_out = product(cosine_table, real_in, pattern) + product(sine_table, imag_in, pattern)
    imag_out = product(cosine_table, imag_in, pattern) - product(sine_table, real_in, pattern)
    return (real_out, imag_out)


def inverse_first(real_in, imag_in, groups):
    length = real_in.shape[1]
    cosine_table, sine_table = phase_table(length, length, length, 0)
    cosine_table = cosine_table.reshape(groups, length // groups, length)
    sine_table = sine_table.reshape(groups, length // groups, length)
    pattern = "gjm,amw->gajw"
    real_out = product(cosine_table, real_in, pattern) - product(sine_table, imag_in, pattern)
    imag_out = product(cosine_table, imag_in, pattern) + product(sine_table, real_in, pattern)
    return jnp.stack([real_out, imag_out], axis=3)


def inverse_second(spectral, offset, period, blocks):
    slab_rows = spectral.shape[1]
    twist_cos, twist_sin = phase_table(2 * blocks, slab_rows, period, offset)
    twist_cos = twist_cos[:, :, None]
    twist_sin = twist_sin[:, :, None]
    real_in = spectral[:, :, 0]
    imag_in = spectral[:, :, 1]
    real_turn = real_in * twist_cos - imag_in * twist_sin
    imag_turn = real_in * twist_sin + imag_in * twist_cos
    cosine_table, sine_table = phase_table(blocks, 2 * blocks, 2 * blocks, 0)
    pattern = "nk,kjw->njw"
    return (product(cosine_table, real_turn, pattern) - product(sine_table, imag_turn, pattern)) * (
        1.0 / period
    )


def transpose(values):
    return lax.all_to_all(values, "seq", split_axis=0, concat_axis=1, tiled=True)


def monarch_forward(signal):
    length, channels = signal.shape
    blocks = lax.axis_size("seq")
    slab_rows = length // blocks
    offset = lax.axis_index("seq") * slab_rows
    arrived = transpose(signal.reshape(blocks, 1, slab_rows, channels)).reshape(
        blocks, slab_rows, channels
    )
    return forward_second(transpose(forward_first(arrived, offset, 2 * blocks * length)))


def monarch_inverse(real_in, imag_in):
    length = real_in.shape[1]
    channels = real_in.shape[2]
    blocks = lax.axis_size("seq")
    slab_rows = length // blocks
    offset = lax.axis_index("seq") * slab_rows
    spectral = transpose(inverse_first(real_in, imag_in, blocks)).reshape(
        2 * blocks, slab_rows, 2, channels
    )
    values = inverse_second(spectral, offset, 2 * blocks * length, blocks)
    return transpose(values.reshape(blocks, 1, slab_rows, channels)).reshape(length, channels)


def complex_mul(left_re, left_im, right_re, right_im):
    return (left_re * right_re - left_im * right_im, left_re * right_im + left_im * right_re)


def conj_mul(left_re, left_im, right_re, right_im):
    return (left_re * right_re + left_im * right_im, left_re * right_im - left_im * right_re)


def group_sum(values, groups):
    return values.reshape(values.shape[:-1] + (values.shape[-1] // groups, groups)).sum(axis=-2)


def causal_taps(signal, previous, tap_weights):
    margin = previous.shape[0]
    length = signal.shape[0]
    extended = jnp.concatenate([previous.astype(jnp.float32), signal.astype(jnp.float32)], axis=0)
    summed = tap_weights[0] * extended[margin : margin + length]
    for shift_by in range(1, tap_weights.shape[0]):
        summed = (
            summed
            + tap_weights[shift_by] * extended[margin - shift_by : margin - shift_by + length]
        )
    return summed


def anticausal_taps(signal, following, tap_weights):
    length = signal.shape[0]
    extended = jnp.concatenate([signal, following], axis=0)
    summed = tap_weights[0] * signal
    for shift_by in range(1, tap_weights.shape[0]):
        summed = summed + tap_weights[shift_by] * extended[shift_by : shift_by + length]
    return summed


def per_device(query_rows, key_rows, value_rows, short_taps, long_filter, cotangent):
    length, channels = query_rows.shape
    groups = long_filter.shape[1]
    margin = short_taps.shape[1] - 1
    lead_query, lead_key, lead_value = shifted(
        (query_rows[length - margin :], key_rows[length - margin :], value_rows[length - margin :]),
        "seq",
        1,
    )
    query_conv = causal_taps(query_rows, lead_query, short_taps[0])
    key_conv = causal_taps(key_rows, lead_key, short_taps[1])
    value_conv = causal_taps(value_rows, lead_value, short_taps[2])
    gated_rows = key_conv * value_conv
    incoming = cotangent.astype(jnp.float32)
    conv_grad = incoming * query_conv
    spec_re, spec_im = monarch_forward(jnp.concatenate([gated_rows, long_filter], axis=1))
    gated_re, gated_im = (spec_re[:, :, :channels], spec_im[:, :, :channels])
    filter_re = jnp.tile(spec_re[:, :, channels : channels + groups], (1, 1, channels // groups))
    filter_im = jnp.tile(spec_im[:, :, channels : channels + groups], (1, 1, channels // groups))
    prod_re, prod_im = complex_mul(gated_re, gated_im, filter_re, filter_im)
    long_conv = monarch_inverse(prod_re, prod_im)
    grad_re, grad_im = monarch_forward(conv_grad)
    back_re, back_im = conj_mul(filter_re, filter_im, grad_re, grad_im)
    cross_re, cross_im = conj_mul(gated_re, gated_im, grad_re, grad_im)
    combined = monarch_inverse(
        jnp.concatenate([back_re, cross_re], axis=2), jnp.concatenate([back_im, cross_im], axis=2)
    )
    gated_grad = combined[:, :channels]
    filter_local = group_sum(combined[:, channels:], groups)
    hyena_out = (query_conv * long_conv).astype(jnp.bfloat16)
    query_grad = incoming * long_conv
    grad_filter = lax.psum(filter_local, "chan")
    key_grad = gated_grad * value_conv
    value_grad = gated_grad * key_conv
    next_query, next_key, next_value = shifted(
        (query_grad[:margin], key_grad[:margin], value_grad[:margin]), "seq", -1
    )
    grad_query = anticausal_taps(query_grad, next_query, short_taps[0]).astype(jnp.bfloat16)
    grad_key = anticausal_taps(key_grad, next_key, short_taps[1]).astype(jnp.bfloat16)
    grad_value = anticausal_taps(value_grad, next_value, short_taps[2]).astype(jnp.bfloat16)
    return (hyena_out, grad_query, grad_key, grad_value, grad_filter)


def solution(mesh):
    in_specs = (
        P("seq", "chan"),
        P("seq", "chan"),
        P("seq", "chan"),
        P(None, None, "chan"),
        P("seq", None),
        P("seq", "chan"),
    )
    out_specs = (
        P("seq", "chan"),
        P("seq", "chan"),
        P("seq", "chan"),
        P("seq", "chan"),
        P("seq", None),
    )
    return jax.shard_map(
        per_device, mesh=mesh, in_specs=in_specs, out_specs=out_specs, check_vma=False
    )
```

profile of v0, /device:TPU:1, one launch (start us, length us, event | category | flops | bytes accessed | tf_op | source)
XLA Modules:
  0.0 750.0 jit_solution(9910461660654692560)
XLA Ops:
  7.9 20.4 %collective-permute-start = (bf16[2,256]{1,0:T(2,128)(2,1)S(1)}, bf16[2,256]{1,0:T(2,128)(2,1)S(1)}, u32[]{:S(2)}, u32[]{:S(2)}) collective-permute-start(bf16[2,256]{1,0:T(2,128)(2,1)S(1)} %slice.158), channel_id=1, source_target_pairs={{0,32},{32,64},{64,96},{96,128},{128,160},{160,192},{192,224},{224... | collective-permute-start | bytes 3080 | tf_op jit(solution)/shard_map/ppermute | solution.py:12
  28.3 0.9 fusion.289
  29.2 0.9 convert_element_type.104
  30.9 17.1 %all-to-all-start.4 = ((f32[32,1,4,256]{3,2,1,0:T(4,128)}), f32[32,1,4,256]{3,2,1,0:T(4,128)S(1)}, u32[]{:S(2)}, u32[]{:S(2)}) async-start(f32[32,1,4,256]{3,2,1,0:T(4,128)} %bitcast.43), calls=%async_computation.4 | async-start | bytes 262144 | tf_op jit(solution)/shard_map/all_to_all | solution.py:84
  48.0 12.3 %collective-permute-start.1 = (bf16[2,256]{1,0:T(2,128)(2,1)S(1)}, bf16[2,256]{1,0:T(2,128)(2,1)S(1)}, u32[]{:S(2)}, u32[]{:S(2)}) collective-permute-start(bf16[2,256]{1,0:T(2,128)(2,1)S(1)} %slice.164), channel_id=1, source_target_pairs={{0,32},{32,64},{64,96},{96,128},{128,160},{160,192},{192,224},{224... | collective-permute-start | bytes 3080 | tf_op jit(solution)/shard_map/ppermute | solution.py:12
  60.3 2.0 collective-permute-start.2
  62.4 1.0 collective-permute-done.2
  63.4 0.7 copy-done.3
  64.2 0.7 reshape.171
  65.5 16.8 %all-to-all-start = ((f32[32,1,4,384]{3,2,1,0:T(4,128)}), f32[32,1,4,384]{3,2,1,0:T(4,128)S(1)}, u32[]{:S(2)}, u32[]{:S(2)}) async-start(f32[32,1,4,384]{3,2,1,0:T(4,128)} %bitcast.11), calls=%async_computation | async-start | bytes 393216 | tf_op jit(solution)/shard_map/all_to_all | solution.py:84
  83.5 1.1 copy.65
  84.7 15.7 %all-to-all-done = f32[32,1,4,384]{3,2,1,0:T(4,128)S(1)} async-done(((f32[32,1,4,384]{3,2,1,0:T(4,128)}), f32[32,1,4,384]{3,2,1,0:T(4,128)S(1)}, u32[]{:S(2)}, u32[]{:S(2)}) %all-to-all-start) | async-done | bytes 196640 | tf_op jit(solution)/shard_map/all_to_all | solution.py:84
  100.4 4.7 all-to-all-start.5
  106.5 1.4 copy.50
  107.9 18.0 %all-to-all-done.5 = f32[64,4,2,256]{3,1,2,0:T(4,128)S(1)} async-done(((f32[64,4,2,256]{3,1,2,0:T(4,128)}), f32[64,4,2,256]{3,1,2,0:T(4,128)S(1)}, u32[]{:S(2)}, u32[]{:S(2)}) %all-to-all-start.5) | async-done | bytes 524320 | tf_op jit(solution)/shard_map/all_to_all | solution.py:84
  125.9 15.9 %all-to-all-start.1 = ((f32[64,4,2,384]{3,1,2,0:T(4,128)}), f32[64,4,2,384]{3,1,2,0:T(4,128)S(1)}, u32[]{:S(2)}, u32[]{:S(2)}) async-start(f32[64,4,2,384]{3,1,2,0:T(4,128)} %copy.50), calls=%async_computation.1 | async-start | bytes 1572864 | tf_op jit(solution)/shard_map/all_to_all | solution.py:84
  144.7 40.9 %all-to-all-done.1 = f32[64,4,2,384]{3,1,2,0:T(4,128)S(1)} async-done(((f32[64,4,2,384]{3,1,2,0:T(4,128)}), f32[64,4,2,384]{3,1,2,0:T(4,128)S(1)}, u32[]{:S(2)}, u32[]{:S(2)}) %all-to-all-start.1) | async-done | bytes 786464 | tf_op jit(solution)/shard_map/all_to_all | solution.py:84
  187.0 0.7 fusion.23
  188.1 0.7 fusion.19
  188.8 0.7 fusion.3
  189.6 0.7 fusion.2
  190.3 0.7 multiply_add_fusion
  193.9 1.1 copy.58
  195.1 4.9 all-to-all-start.2
  199.9 1.0 fusion.18
  200.9 0.9 fusion.1
  201.8 0.9 fusion.17
  202.8 0.9 fusion
  203.8 1.6 copy.73
  205.5 20.6 %all-to-all-done.2 = f32[32,2,4,2,256]{4,2,1,3,0:T(4,128)S(1)} async-done(((f32[32,2,4,2,256]{4,2,1,3,0:T(4,128)}), f32[32,2,4,2,256]{4,2,1,3,0:T(4,128)S(1)}, u32[]{:S(2)}, u32[]{:S(2)}) %all-to-all-start.2) | async-done | bytes 524320 | tf_op jit(solution)/shard_map/all_to_all | solution.py:84
  226.0 4.9 all-to-all-start.6
  232.8 0.7 copy.62
  233.6 45.1 %all-to-all-done.6 = f32[32,2,4,2,512]{4,2,1,3,0:T(4,128)S(1)} async-done(((f32[32,2,4,2,512]{4,2,1,3,0:T(4,128)}), f32[32,2,4,2,512]{4,2,1,3,0:T(4,128)S(1)}, u32[]{:S(2)}, u32[]{:S(2)}) %all-to-all-start.6) | async-done | bytes 1048608 | tf_op jit(solution)/shard_map/all_to_all | solution.py:84
  278.7 11.4 %all-to-all-start.3 = ((f32[32,1,4,256]{3,2,1,0:T(4,128)}), f32[32,1,4,256]{3,2,1,0:T(4,128)S(1)}, u32[]{:S(2)}, u32[]{:S(2)}) async-start(f32[32,1,4,256]{3,2,1,0:T(4,128)} %copy.62), calls=%async_computation.3 | async-start | bytes 262144 | tf_op jit(solution)/shard_map/all_to_all | solution.py:84
  290.1 0.8 copy.74
  291.0 0.8 fusion.284
  293.3 0.9 copy.80
  294.1 13.3 %all-to-all-done.3 = f32[32,1,4,256]{3,2,1,0:T(4,128)S(1)} async-done(((f32[32,1,4,256]{3,2,1,0:T(4,128)}), f32[32,1,4,256]{3,2,1,0:T(4,128)S(1)}, u32[]{:S(2)}, u32[]{:S(2)}) %all-to-all-start.3) | async-done | bytes 131104 | tf_op jit(solution)/shard_map/all_to_all | solution.py:84
  307.4 4.2 all-to-all-start.7
  312.3 2.1 collective-permute-start.3
  314.5 15.5 %all-to-all-done.7 = f32[32,1,4,512]{3,2,1,0:T(4,128)S(1)} async-done(((f32[32,1,4,512]{3,2,1,0:T(4,128)}), f32[32,1,4,512]{3,2,1,0:T(4,128)S(1)}, u32[]{:S(2)}, u32[]{:S(2)}) %all-to-all-start.7) | async-done | bytes 262176 | tf_op jit(solution)/shard_map/all_to_all | solution.py:84
  330.1 2.3 collective-permute-start.5
  333.2 0.8 reduce_sum.9
  334.1 1.9 collective-permute-start.4
  336.0 7.8 %collective-permute-done.5 = f32[2,256]{1,0:T(2,128)S(1)} collective-permute-done((f32[2,256]{1,0:T(2,128)S(1)}, f32[2,256]{1,0:T(2,128)S(1)}, u32[]{:S(2)}, u32[]{:S(2)}) %collective-permute-start.5) | collective-permute-done | bytes 2080 | tf_op jit(solution)/shard_map/ppermute | solution.py:12
  344.4 3.2 collective-permute-done.4
  348.4 393.3 %all-reduce.2.cloned.1.call-done = f32[128,128]{1,0:T(8,128)} async-done(((f32[128,128]{1,0:T(8,128)}), f32[128,128]{1,0:T(8,128)}) %all-reduce.2.cloned.1.call-update) | async-done | bytes 65552 | tf_op jit(solution)/shard_map/psum | solution.py:176
  741.7 1.5 copy.159
  (73 shorter events, 18.5 us)
Async XLA Ops:
  7.9 22.2 %collective-permute-start = (bf16[2,256]{1,0:T(2,128)(2,1)S(1)}, bf16[2,256]{1,0:T(2,128)(2,1)S(1)}, u32[]{:S(2)}, u32[]{:S(2)}) collective-permute-start(bf16[2,256]{1,0:T(2,128)(2,1)S(1)} %slice.158), channel_id=1, source_target_pairs={{0,32},{32,64},{64,96},{96,128},{128,160},{160,192},{192,224},{224... | collective-permute-start | bytes 3080 | tf_op jit(solution)/shard_map/ppermute | solution.py:12
  29.2 0.9 copy-start
  30.9 17.1 %copy-start.1 = (bf16[128,256]{1,0:T(8,128)(2,1)S(1)}, bf16[128,256]{1,0:T(8,128)(2,1)}, u32[]{:S(2)}) copy-start(bf16[128,256]{1,0:T(8,128)(2,1)} %param.7) | copy-start | bytes 196612
  30.9 29.4 %copy-start.2 = (bf16[128,256]{1,0:T(8,128)(2,1)S(1)}, bf16[128,256]{1,0:T(8,128)(2,1)}, u32[]{:S(2)}) copy-start(bf16[128,256]{1,0:T(8,128)(2,1)} %param.8) | copy-start | bytes 196612
  30.9 34.6 %all-to-all-start.4 = ((f32[32,1,4,256]{3,2,1,0:T(4,128)}), f32[32,1,4,256]{3,2,1,0:T(4,128)S(1)}, u32[]{:S(2)}, u32[]{:S(2)}) async-start(f32[32,1,4,256]{3,2,1,0:T(4,128)} %bitcast.43), calls=%async_computation.4 | async-start | bytes 262144 | tf_op jit(solution)/shard_map/all_to_all | solution.py:84
  48.0 14.4 %collective-permute-start.1 = (bf16[2,256]{1,0:T(2,128)(2,1)S(1)}, bf16[2,256]{1,0:T(2,128)(2,1)S(1)}, u32[]{:S(2)}, u32[]{:S(2)}) collective-permute-start(bf16[2,256]{1,0:T(2,128)(2,1)S(1)} %slice.164), channel_id=1, source_target_pairs={{0,32},{32,64},{64,96},{96,128},{128,160},{160,192},{192,224},{224... | collective-permute-start | bytes 3080 | tf_op jit(solution)/shard_map/ppermute | solution.py:12
  60.3 3.1 collective-permute-start.2
  63.4 0.8 copy-start.3
  65.5 35.0 %all-to-all-start = ((f32[32,1,4,384]{3,2,1,0:T(4,128)}), f32[32,1,4,384]{3,2,1,0:T(4,128)S(1)}, u32[]{:S(2)}, u32[]{:S(2)}) async-start(f32[32,1,4,384]{3,2,1,0:T(4,128)} %bitcast.11), calls=%async_computation | async-start | bytes 393216 | tf_op jit(solution)/shard_map/all_to_all | solution.py:84
  100.4 25.5 %all-to-all-start.5 = ((f32[64,4,2,256]{3,1,2,0:T(4,128)}), f32[64,4,2,256]{3,1,2,0:T(4,128)S(1)}, u32[]{:S(2)}, u32[]{:S(2)}) async-start(f32[64,4,2,256]{3,1,2,0:T(4,128)} %copy.65), calls=%async_computation.5 | async-start | bytes 1048576 | tf_op jit(solution)/shard_map/all_to_all | solution.py:84
  125.9 59.7 %all-to-all-start.1 = ((f32[64,4,2,384]{3,1,2,0:T(4,128)}), f32[64,4,2,384]{3,1,2,0:T(4,128)S(1)}, u32[]{:S(2)}, u32[]{:S(2)}) async-start(f32[64,4,2,384]{3,1,2,0:T(4,128)} %copy.50), calls=%async_computation.1 | async-start | bytes 1572864 | tf_op jit(solution)/shard_map/all_to_all | solution.py:84
  195.1 31.0 %all-to-all-start.2 = ((f32[32,2,4,2,256]{4,2,1,3,0:T(4,128)}), f32[32,2,4,2,256]{4,2,1,3,0:T(4,128)S(1)}, u32[]{:S(2)}, u32[]{:S(2)}) async-start(f32[32,2,4,2,256]{4,2,1,3,0:T(4,128)} %copy.58), calls=%async_computation.2 | async-start | bytes 1048576 | tf_op jit(solution)/shard_map/all_to_all | solution.py:84
  226.0 52.6 %all-to-all-start.6 = ((f32[32,2,4,2,512]{4,2,1,3,0:T(4,128)}), f32[32,2,4,2,512]{4,2,1,3,0:T(4,128)S(1)}, u32[]{:S(2)}, u32[]{:S(2)}) async-start(f32[32,2,4,2,512]{4,2,1,3,0:T(4,128)} %copy.73), calls=%async_computation.6 | async-start | bytes 2097152 | tf_op jit(solution)/shard_map/all_to_all | solution.py:84
  278.7 28.7 %all-to-all-start.3 = ((f32[32,1,4,256]{3,2,1,0:T(4,128)}), f32[32,1,4,256]{3,2,1,0:T(4,128)S(1)}, u32[]{:S(2)}, u32[]{:S(2)}) async-start(f32[32,1,4,256]{3,2,1,0:T(4,128)} %copy.62), calls=%async_computation.3 | async-start | bytes 262144 | tf_op jit(solution)/shard_map/all_to_all | solution.py:84
  307.4 22.6 %all-to-all-start.7 = ((f32[32,1,4,512]{3,2,1,0:T(4,128)}), f32[32,1,4,512]{3,2,1,0:T(4,128)S(1)}, u32[]{:S(2)}, u32[]{:S(2)}) async-start(f32[32,1,4,512]{3,2,1,0:T(4,128)} %copy.80), calls=%async_computation.7 | async-start | bytes 524288 | tf_op jit(solution)/shard_map/all_to_all | solution.py:84
  311.6 430.1 %all-reduce.2.cloned.1.call-start = ((), (), s32[]{:S(2)}) async-start(), calls=%async_computation.8 | async-start | bytes 131072 | tf_op jit(solution)/shard_map/psum | solution.py:176
  312.3 20.1 %collective-permute-start.3 = (f32[2,256]{1,0:T(2,128)S(1)}, f32[2,256]{1,0:T(2,128)S(1)}, u32[]{:S(2)}, u32[]{:S(2)}) collective-permute-start(f32[2,256]{1,0:T(2,128)S(1)} %slice.211), channel_id=1, source_target_pairs={{32,0},{64,32},{96,64},{128,96},{160,128},{192,160},{224,192},{256... | collective-permute-start | bytes 6152 | tf_op jit(solution)/shard_map/ppermute | solution.py:12
  330.1 13.6 %collective-permute-start.5 = (f32[2,256]{1,0:T(2,128)S(1)}, f32[2,256]{1,0:T(2,128)S(1)}, u32[]{:S(2)}, u32[]{:S(2)}) collective-permute-start(f32[2,256]{1,0:T(2,128)S(1)} %slice.222), channel_id=1, source_target_pairs={{32,0},{64,32},{96,64},{128,96},{160,128},{192,160},{224,192},{256... | collective-permute-start | bytes 6152 | tf_op jit(solution)/shard_map/ppermute | solution.py:12
  334.1 13.6 %collective-permute-start.4 = (f32[2,256]{1,0:T(2,128)S(1)}, f32[2,256]{1,0:T(2,128)S(1)}, u32[]{:S(2)}, u32[]{:S(2)}) collective-permute-start(f32[2,256]{1,0:T(2,128)S(1)} %slice.219), channel_id=1, source_target_pairs={{32,0},{64,32},{96,64},{128,96},{160,128},{192,160},{224,192},{256... | collective-permute-start | bytes 6152 | tf_op jit(solution)/shard_map/ppermute | solution.py:12
Sparse Core Ops, SparseCore 0:
  334.2 407.4 all-reduce.1
where the time goes:
time: 760 us; the launch traced here: 750 us
  waiting for transfers between devices  575 us (76%)
  starting transfers between devices  121 us (16%)
  local copies, waits for them, and re-layouts  17.6 us (2%)
  matrix products  16.4 us (2%)
  between operations  14.7 us (2%)
    psum x1, waiting for transfers between devices, per_device(): grad_filter = lax.psum(filter_local, 'chan')  393 us
    all_to_all x8, waiting for transfers between devices, transpose(): lax.all_to_all(values, 'seq', split_axis=0, concat_axis=1, tiled=True)  170 us
    all_to_all x8, starting transfers between devices, transpose(): lax.all_to_all(values, 'seq', split_axis=0, concat_axis=1, tiled=True)  80 us
    ppermute x6, starting transfers between devices, shifted(): return lax.ppermute(block, axis, route)  41.1 us
    dot_general x24, matrix products, product(): return jnp.einsum(pattern, matrix, operand, precision=lax.Precision.HIGHEST)  16.4 us
  transfers between devices with their start and end apart: 15, of which 12 were waited for; matrix products, arithmetic and copies ran while one was open for 3% of the time, Pallas kernels for 0%

commit v1 on v0

v1 whole, which is shorter than its diff:
```python
import functools

import jax
import jax.numpy as jnp
import ml_dtypes
import numpy as np
from jax import lax
from jax.experimental import pallas as pl
from jax.experimental.pallas import tpu as pltpu
from jax.sharding import PartitionSpec as P

F32 = jnp.float32
BF16 = jnp.bfloat16


def halves(table):
    high = table.astype(ml_dtypes.bfloat16)
    low = (table - high.astype(np.float64)).astype(ml_dtypes.bfloat16)
    return high, low


def tables(blocks, slab, per):
    outer = 2 * blocks
    period = outer * slab
    bins = blocks + 2
    k1 = np.arange(bins)[:, None]
    used = (k1 <= blocks).astype(np.float64)
    angle = 2 * np.pi * (k1 * np.arange(blocks)[None, :] % outer) / outer
    cosine, sine = np.cos(angle), np.sin(angle)
    eye = np.eye(per)
    first = np.concatenate([np.kron(cosine * used, eye), np.kron(-sine * used, eye)], axis=0)
    weight = used * np.where((k1 == 0) | (k1 == blocks), 1.0, 2.0) / period
    last = np.kron((cosine * weight).T, eye), np.kron((-sine * weight).T, eye)
    turn = 2 * np.pi * (k1 * np.arange(slab)[None, :] % period) / period
    twist_re = np.repeat(np.cos(turn), per, axis=0).astype(np.float32)
    twist_im = np.repeat(-np.sin(turn), per, axis=0).astype(np.float32)
    spin = 2 * np.pi * (np.arange(slab)[:, None] * np.arange(slab)[None, :] % slab) / slab
    c, s = np.cos(spin), np.sin(spin)
    ahead = np.block([[c, -s], [s, c]])
    back = np.block([[c, s], [-s, c]])
    out = []
    for table in (first, ahead, back, np.concatenate(last, axis=1)):
        out.extend(halves(table))
    return out + [twist_re, twist_im]


def orders(blocks, channels):
    half = channels // 2
    i_size = half // blocks
    row = np.arange(channels)
    d, h, i = row // (2 * i_size), row // i_size % 2, row % i_size
    pick = np.zeros((channels, channels), ml_dtypes.bfloat16)
    pick[row, h * half + d * i_size + i] = 1
    fold = np.zeros((channels, half), ml_dtypes.bfloat16)
    fold[row, d * i_size + i] = 1
    return pick, fold


def dot(left, right, dims=((1,), (0,))):
    return lax.dot_general(left, right, (dims, ((), ())), preferred_element_type=F32)


def split(values):
    high = values.astype(BF16)
    return high, (values - high.astype(F32)).astype(BF16)


def unpack_kernel(in_ref, share_ref, pick_ref, fold_ref, h_ref, q_ref, k_ref, v_ref, f_ref):
    arrived = in_ref[...].astype(F32)
    share = share_ref[...].astype(F32)
    blocks, per, slab = share.shape
    pick = pick_ref[...]

    def flat(part):
        return part.reshape(blocks * per, slab).astype(BF16)

    for p, ref in enumerate((h_ref, q_ref, k_ref, v_ref)):
        ref[...] = dot(flat(arrived[:, p * per : (p + 1) * per]), pick, ((0,), (0,))).astype(BF16)
    f_ref[...] = dot(flat(share), fold_ref[...], ((0,), (0,)))


def shift(values, distance):
    slab = values.shape[2]
    lane = lax.broadcasted_iota(jnp.int32, values.shape, 2)
    turned = pltpu.roll(values, distance % slab, 2)
    edge = jnp.zeros((1,) + values.shape[1:], values.dtype)
    if distance > 0:
        return jnp.where(lane < distance, jnp.concatenate([edge, turned[:-1]], axis=0), turned)
    return jnp.where(lane >= slab + distance, jnp.concatenate([turned[1:], edge], axis=0), turned)


def taps(values, weights, sign):
    total = weights[0] * values
    for j in range(1, len(weights)):
        total = total + weights[j] * shift(values, sign * j)
    return total


RUN = 8


class Place:
    def __init__(self):
        self.seq, self.chan = lax.axis_index("seq"), lax.axis_index("chan")
        self.blocks, self.columns = lax.axis_size("seq"), lax.axis_size("chan")
        self.run = min(RUN, self.columns)
        self.work_seq, self.work_chan = self.moved(self.seq, self.chan, 2 * self.run - self.run // 2)

    def moved(self, seq, chan, distance):
        run = self.run
        z = (seq // 2 % 2 * run + chan % run + distance) % (2 * run)
        return seq // 4 * 4 + z // run * 2 + seq % 2, chan // run * run + z % run

    def worker(self, seq, chan):
        return self.moved(seq, chan, self.run // 2)

    def member(self, step):
        rows = self.blocks // 4
        row = (self.seq // 4 + step // 4 + rows // 2) % rows
        return row * 4 + (self.seq + step) % 4


def loop(count, act):
    def body(step, carry):
        act(step)
        return carry

    lax.fori_loop(0, count, body, 0)


def device(pair):
    return {"device_id": {"seq": pair[0], "chan": pair[1]}, "device_id_type": pl.DeviceIdType.MESH}


def whole_kernel(
    q_hbm, k_hbm, v_hbm, f_hbm, ct_hbm, taps_hbm, pick_hbm,
    first_hi_hbm, first_lo_hbm, ahead_hi_hbm, ahead_lo_hbm, back_hi_hbm, back_lo_hbm, last_hi_hbm, last_lo_hbm,
    twist_re_hbm, twist_im_hbm,
    out_ref, share_ref,
    q_ref, k_ref, v_ref, f_ref, ct_ref, taps_ref, pick_ref,
    first_hi, first_lo, ahead_hi, ahead_lo, back_hi, back_lo, last_hi, last_lo,
    twist_re_ref, twist_im_ref,
    packed, held, done, returned, cross_out, cross_in, total, shares,
    load_sems, send_sems, recv_sems,
):
    here = Place()
    count = here.columns
    barrier = pltpu.get_barrier_semaphore()
    blocks, rows, slab = packed.shape
    per = rows // 5
    alone = here.work_chan == here.seq

    def greet(pair):
        pl.semaphore_signal(barrier, inc=1, **device(pair))

    def towards(step):
        return (here.work_chan + 1 + step) % count

    def other(step):
        return (here.work_seq + 1 + step) % blocks

    loop(blocks, lambda step: greet((here.member(step), here.work_chan)))
    loop(blocks - 1, lambda step: greet(here.worker(other(step), here.seq)))
    pl.when(jnp.logical_not(alone))(lambda: greet(here.worker(here.work_seq, here.seq)))
    loop(count - 1, lambda step: greet(here.worker(here.work_seq, towards(step))))

    pairs = [
        (q_hbm, q_ref), (k_hbm, k_ref), (v_hbm, v_ref), (f_hbm, f_ref), (ct_hbm, ct_ref), (pick_hbm, pick_ref),
        (first_hi_hbm, first_hi), (first_lo_hbm, first_lo), (ahead_hi_hbm, ahead_hi),
        (ahead_lo_hbm, ahead_lo), (back_hi_hbm, back_hi), (back_lo_hbm, back_lo), (last_hi_hbm, last_hi),
        (last_lo_hbm, last_lo), (twist_re_hbm, twist_re_ref), (twist_im_hbm, twist_im_ref),
    ]
    loads = [pltpu.make_async_copy(source, local, load_sems.at[i]) for i, (source, local) in enumerate(pairs)]
    for load in loads:
        load.start()
    for load in loads[:6]:
        load.wait()

    high, low = split(f_ref[...])
    pick = pick_ref[...]
    parts = []
    for values in (q_ref[...], k_ref[...], v_ref[...], ct_ref[...], jnp.concatenate([high, low], axis=1)):
        parts.append(dot(pick, values, ((1,), (1,))).reshape(blocks, per, slab))
    packed[...] = jnp.concatenate(parts, axis=1).astype(BF16)

    def remote(number, source, target, pair):
        return pltpu.make_async_remote_copy(
            src_ref=source, dst_ref=target,
            send_sem=send_sems.at[number], recv_sem=recv_sems.at[number], **device(pair),
        )

    def bring(step):
        to = here.member(step)
        remote(0, packed.at[to], held.at[here.seq], here.worker(to, here.chan)).start()

    def give(step):
        to = here.member(step)
        remote(1, done.at[to], returned.at[here.work_seq], (to, here.work_chan)).start()

    def scatter(step):
        to = towards(step)
        place = here.worker(here.work_seq, to)
        remote(2, cross_out.at[to], cross_in.at[here.work_chan], place).start()

    def spread(step):
        to = (here.chan + 1 + step) % count
        remote(3, total.at[0], shares.at[here.work_seq], (here.work_chan, to)).start()

    origin = here.worker(here.seq, here.chan)
    pl.semaphore_wait(barrier, blocks + count - 1 + blocks - jnp.where(alone, 1, 0))
    taps_copy = remote(4, taps_hbm, taps_ref, origin)
    taps_copy.start()
    loop(blocks, bring)
    for load in loads[6:]:
        load.wait()
    taps_copy.wait_recv()
    channels = pick.shape[0]
    row = lax.broadcasted_iota(jnp.int32, (per, channels), 0)
    column = lax.broadcasted_iota(jnp.int32, (per, channels), 1)
    wanted = jnp.where(row < per // 2, row, row + (channels - per) // 2) + here.work_seq * (per // 2)
    choice = jnp.where(column == wanted, 1.0, 0.0).astype(F32)
    weights = []
    for p in range(3):
        own = lax.dot_general(
            choice, taps_ref[p], (((1,), (1,)), ((), ())),
            precision=lax.Precision.HIGHEST, preferred_element_type=F32,
        )
        weights.append([own[:, j : j + 1].reshape(1, per, 1) for j in range(own.shape[1])])

    remote(0, packed, held, origin).wait_recv()

    arrived = held[...].astype(F32)
    q, k, v, incoming, filt = (arrived[:, p * per : (p + 1) * per] for p in range(5))
    query_conv = taps(q, weights[0], 1)
    key_conv = taps(k, weights[1], 1)
    value_conv = taps(v, weights[2], 1)
    gated = (key_conv * value_conv).reshape(blocks * per, slab)
    conv_grad = (incoming * query_conv).reshape(blocks * per, slab)

    twist_re, twist_im = twist_re_ref[...], twist_im_ref[...]
    bins = twist_re.shape[0]

    def triple(left_hi, left_lo, right_hi, right_lo):
        return dot(left_hi, right_hi) + (dot(left_hi, right_lo) + dot(left_lo, right_hi))

    def finish(real, imag):
        turned = jnp.concatenate(
            [real * twist_re - imag * twist_im, real * twist_im + imag * twist_re], axis=1
        )
        spec = triple(*split(turned), ahead_hi[...], ahead_lo[...])
        return spec[:, :slab], spec[:, slab:]

    def inverse(real, imag):
        spec = triple(*split(jnp.concatenate([real, imag], axis=1)), back_hi[...], back_lo[...])
        real, imag = spec[:, :slab], spec[:, slab:]
        return jnp.concatenate(
            [real * twist_re + imag * twist_im, imag * twist_re - real * twist_im], axis=0
        )

    def halved(values):
        row = lax.broadcasted_iota(jnp.int32, values.shape, values.ndim - 2)
        high = values.astype(BF16).astype(F32)
        return jnp.where(row < per // 2, high, values - high).astype(BF16)

    high, low = split(jnp.concatenate([gated, conv_grad], axis=1))
    both = triple(first_hi[...], first_lo[...], high, low)
    g_re, g_im = finish(both[:bins, :slab], both[bins:, :slab])
    c_re, c_im = finish(both[:bins, slab:], both[bins:, slab:])
    cross = inverse(g_re * c_re + g_im * c_im, g_re * c_im - g_im * c_re)
    cross = triple(last_hi[...], last_lo[...], *split(cross)).reshape(blocks, per, slab)
    cross_out[...] = halved(cross + pltpu.roll(cross, per // 2, 1))

    own = (filt + pltpu.roll(filt, per // 2, 1)).reshape(blocks * per, slab)
    own = triple(first_hi[...], first_lo[...], *split(own))
    f_re, f_im = finish(own[:bins], own[bins:])
    loop(count - 1, scatter)
    kept = pltpu.make_async_copy(cross_out.at[here.work_chan], cross_in.at[here.work_chan], recv_sems.at[2])
    kept.start()
    long = inverse(g_re * f_re - g_im * f_im, g_re * f_im + g_im * f_re)
    back = inverse(f_re * c_re + f_im * c_im, f_re * c_im - f_im * c_re)
    wide = triple(last_hi[...], last_lo[...], *split(jnp.concatenate([long, back], axis=1)))
    long_conv = wide[:, :slab].reshape(blocks, per, slab)
    gated_grad = wide[:, slab:].reshape(blocks, per, slab)
    parts = [
        query_conv * long_conv,
        taps(incoming * long_conv, weights[0], -1),
        taps(gated_grad * value_conv, weights[1], -1),
        taps(gated_grad * key_conv, weights[2], -1),
    ]
    done[...] = jnp.concatenate(parts, axis=1).astype(BF16)
    loop(blocks, give)

    remote(2, cross_out, cross_in, origin).wait_recv()
    summed = jnp.sum(cross_in[...].astype(F32), axis=0, keepdims=True)
    total[...] = halved(summed + pltpu.roll(summed, per // 2, 1))
    loop(count - 1, spread)

    @pl.when(jnp.logical_not(alone))
    def _():
        spread(count - 1)
        remote(3, total.at[0], shares.at[0], origin).wait_send()

    @pl.when(alone)
    def _():
        pltpu.make_async_copy(total.at[0], shares.at[here.work_seq], recv_sems.at[3]).start()

    remote(1, done, returned, origin).wait_recv()
    out_ref[...] = returned[...]
    remote(3, shares, shares, origin).wait_recv()
    share_ref[...] = shares[...]
    taps_copy.wait_send()
    remote(0, packed, held, origin).wait_send()
    remote(1, done, returned, origin).wait_send()
    fewer = pl.ds(0, count - 1)
    remote(2, cross_out.at[fewer], cross_in.at[fewer], origin).wait_send()
    remote(3, shares.at[fewer], shares.at[fewer], origin).wait_send()


def call(body, name, outs, *operands, space=pltpu.VMEM, **more):
    return pl.pallas_call(
        body,
        name=name,
        out_shape=outs,
        in_specs=[pl.BlockSpec(memory_space=space)] * len(operands),
        out_specs=jax.tree.map(lambda _: pl.BlockSpec(memory_space=pltpu.VMEM), outs),
        **more,
    )(*operands)


def whole(query_rows, key_rows, value_rows, long_filter, cotangent, short_taps):
    slab, channels = query_rows.shape
    blocks = lax.axis_size("seq")
    per = channels // blocks
    pick, _ = orders(blocks, channels)
    shape = functools.partial(jax.ShapeDtypeStruct, dtype=BF16)
    operands = [
        query_rows, key_rows, value_rows, long_filter, cotangent, short_taps, pick,
        *tables(blocks, slab, per),
    ]
    small = pltpu.VMEM((blocks, per, slab), BF16)
    return call(
        whole_kernel,
        "whole",
        [shape((blocks, 4 * per, slab)), shape((blocks, per, slab))],
        *operands,
        space=pl.ANY,
        scratch_shapes=[
            *[pltpu.VMEM(x.shape, x.dtype) for x in operands],
            *[pltpu.VMEM((blocks, 5 * per, slab), BF16)] * 2,
            *[pltpu.VMEM((blocks, 4 * per, slab), BF16)] * 2,
            small, small, pltpu.VMEM((1, per, slab), BF16), small,
            pltpu.SemaphoreType.DMA((len(operands) - 1,)),
            *[pltpu.SemaphoreType.DMA((5,))] * 2,
        ],
        compiler_params=pltpu.CompilerParams(collective_id=0, has_side_effects=True),
    )


def unpack(returned, shares):
    blocks, per, slab = shares.shape
    channels = blocks * per
    pick, fold = orders(blocks, channels)
    outs = [jax.ShapeDtypeStruct((slab, channels), BF16)] * 4
    outs.append(jax.ShapeDtypeStruct((slab, channels // 2), F32))
    return call(unpack_kernel, "unpack", outs, returned, shares, pick, fold)


def per_device(query_rows, key_rows, value_rows, short_taps, long_filter, cotangent):
    return tuple(
        unpack(*whole(query_rows, key_rows, value_rows, long_filter, cotangent, short_taps))
    )


def solution(mesh):
    wide = P("seq", "chan")
    in_specs = (wide, wide, wide, P(None, None, "chan"), P("seq", None), wide)
    out_specs = (wide, wide, wide, wide, P("seq", None))
    return jax.shard_map(
        per_device, mesh=mesh, in_specs=in_specs, out_specs=out_specs, check_vma=False
    )
```

time: 760 us -> 74.5 us (0.10); the launches traced: 750 us -> 74.3 us
  waiting for transfers between devices: 575 us -> 0 us
  starting transfers between devices: 121 us -> 0 us
  Pallas kernels: 0 us -> 73.7 us
  local copies, waits for them, and re-layouts: 17.6 us -> 0 us
  matrix products: 16.4 us -> 0 us
  between operations: 14.7 us -> 0.64 us
    psum x1 -> x0, waiting for transfers between devices: 393 us -> none  [per_device(): grad_filter = lax.psum(filter_local, 'chan')]
    all_to_all x8 -> x0, waiting for transfers between devices: 170 us -> none  [transpose(): lax.all_to_all(values, 'seq', split_axis=0, concat_axis=1, tiled=True)]
    all_to_all x8 -> x0, starting transfers between devices: 80 us -> none  [transpose(): lax.all_to_all(values, 'seq', split_axis=0, concat_axis=1, tiled=True)]
    pallas_call x0 -> x2, Pallas kernels: none -> 73.7 us  [call(): pl.pallas_call(body, name=name, out_shape=outs, in_specs=[pl.BlockSpec(me...]
    ppermute x6 -> x0, starting transfers between devices: 41.1 us -> none  [shifted(): return lax.ppermute(block, axis, route)]
    dot_general x24 -> x0, matrix products: 16.4 us -> none  [product(): return jnp.einsum(pattern, matrix, operand, precision=lax.Precision.HIGHEST)]
    ppermute x6 -> x0, waiting for transfers between devices: 12 us -> none  [shifted(): return lax.ppermute(block, axis, route)]
  transfers between devices with their start and end apart: 15 -> 0, of which waited for: 12 -> 0; matrix products, arithmetic and copies ran while one was open for 3% -> 0% of each run, Pallas kernels for 0% -> 0%
where the time goes in v1:
time: 74.5 us; the launch traced here: 74.3 us
  Pallas kernels  73.7 us (99%)
    pallas_call x2, Pallas kernels, call(): pl.pallas_call(body, name=name, out_shape=outs, in_specs=[pl.BlockSpec(me...  73.7 us

profile of v1, /device:TPU:1, one launch (start us, length us, event | category | flops | bytes accessed | tf_op | source)
XLA Modules:
  0.0 74.3 jit_solution(7475367015058330125)
XLA Ops:
  0.6 71.7 %whole.1 = (bf16[32,32,128]{2,1,0:T(8,128)(2,1)}, bf16[32,8,128]{2,1,0:T(8,128)(2,1)}) custom-call(bf16[128,256]{1,0:T(8,128)(2,1)} %q_hbm.1, bf16[128,256]{1,0:T(8,128)(2,1)} %k_hbm.1, bf16[128,256]{1,0:T(8,128)(2,1)} %v_hbm.1, f32[128,128]{1,0:T(8,128)} %f_hbm.1, bf16[128,256]{1,0:T(8,128)(2,1)} %ct_hbm.1, f32[3,3,256]{2,1,0:T(4,128)} %taps_hbm.1, ...), custom_call_target="tpu_custom_call" | custom-call | tf_op jit(solution)/shard_map/whole/pallas_call | solution.py:320
  72.4 2.0 %unpack.1 = (bf16[128,256]{1,0:T(8,128)(2,1)}, bf16[128,256]{1,0:T(8,128)(2,1)}, bf16[128,256]{1,0:T(8,128)(2,1)}, bf16[128,256]{1,0:T(8,128)(2,1)}, f32[128,128]{1,0:T(8,128)}) custom-call(bf16[32,32,128]{2,1,0:T(8,128)(2,1)} %get-tuple-element.7.in_ref, bf16[32,8,128]{2,1,0:T(8,128)(2,1)} %get-tuple-element.8.share_ref, ...), custom_call_target="tpu_custom_call" | custom-call | tf_op jit(solution)/shard_map/unpack/pallas_call | solution.py:320

commit v2 on v1

--- a/solution.py
+++ b/solution.py
@@ -108,24 +108,29 @@
 
     def moved(self, seq, chan, distance):
         run = self.run
-        z = (seq // 2 % 2 * run + chan % run + distance) % (2 * run)
-        return seq // 4 * 4 + z // run * 2 + seq % 2, chan // run * run + z % run
+        far, column = lax.rem(lax.div(seq, 2), 2), lax.rem(chan, run)
+        z = lax.rem(far * run + column + distance, 2 * run)
+        there = lax.div(z, run)
+        return seq + (there - far) * 2, chan - column + z - there * run
 
     def worker(self, seq, chan):
         return self.moved(seq, chan, self.run // 2)
 
     def member(self, step):
         rows = self.blocks // 4
-        row = (self.seq // 4 + step // 4 + rows // 2) % rows
-        return row * 4 + (self.seq + step) % 4
-
-
-def loop(count, act):
-    def body(step, carry):
-        act(step)
+        row = lax.rem(lax.div(self.seq, 4) + lax.div(step, 4) + rows // 2, rows)
+        return row * 4 + lax.rem(self.seq + step, 4)
+
+
+def loop(count, act, width=4):
+    def body(turn, carry):
+        for step in range(width):
+            act(turn * width + step)
         return carry
 
-    lax.fori_loop(0, count, body, 0)
+    lax.fori_loop(0, count // width, body, 0)
+    for step in range(count // width * width, count):
+        act(jnp.int32(step))
 
 
 def device(pair):
@@ -140,29 +145,30 @@
     q_ref, k_ref, v_ref, f_ref, ct_ref, taps_ref, pick_ref,
     first_hi, first_lo, ahead_hi, ahead_lo, back_hi, back_lo, last_hi, last_lo,
     twist_re_ref, twist_im_ref,
-    packed, held, done, returned, cross_out, cross_in, total, shares,
+    packed, packed_late, held, held_late, done, done_late, returned, returned_late,
+    cross_out, cross_in, total, shares,
     load_sems, send_sems, recv_sems,
 ):
     here = Place()
     count = here.columns
     barrier = pltpu.get_barrier_semaphore()
     blocks, rows, slab = packed.shape
-    per = rows // 5
+    per = rows // 4
     alone = here.work_chan == here.seq
 
     def greet(pair):
         pl.semaphore_signal(barrier, inc=1, **device(pair))
 
     def towards(step):
-        return (here.work_chan + 1 + step) % count
+        return lax.rem(here.work_chan + 1 + step, count)
 
     def other(step):
-        return (here.work_seq + 1 + step) % blocks
-
-    loop(blocks, lambda step: greet((here.member(step), here.work_chan)))
+        return lax.rem(here.work_seq + 1 + step, blocks)
+
     loop(blocks - 1, lambda step: greet(here.worker(other(step), here.seq)))
     pl.when(jnp.logical_not(alone))(lambda: greet(here.worker(here.work_seq, here.seq)))
     loop(count - 1, lambda step: greet(here.worker(here.work_seq, towards(step))))
+    loop(blocks, lambda step: greet((here.member(step), here.work_chan)))
 
     pairs = [
         (q_hbm, q_ref), (k_hbm, k_ref), (v_hbm, v_ref), (f_hbm, f_ref), (ct_hbm, ct_ref), (pick_hbm, pick_ref),
@@ -178,10 +184,13 @@
 
     high, low = split(f_ref[...])
     pick = pick_ref[...]
-    parts = []
-    for values in (q_ref[...], k_ref[...], v_ref[...], ct_ref[...], jnp.concatenate([high, low], axis=1)):
-        parts.append(dot(pick, values, ((1,), (1,))).reshape(blocks, per, slab))
-    packed[...] = jnp.concatenate(parts, axis=1).astype(BF16)
+
+    def pack(*parts):
+        parts = [dot(pick, values, ((1,), (1,))).reshape(blocks, per, slab) for values in parts]
+        return jnp.concatenate(parts, axis=1).astype(BF16)
+
+    packed[...] = pack(k_ref[...], v_ref[...], q_ref[...], ct_ref[...])
+    packed_late[...] = pack(jnp.concatenate([high, low], axis=1))
 
     def remote(number, source, target, pair):
         return pltpu.make_async_remote_copy(
@@ -193,9 +202,17 @@
         to = here.member(step)
         remote(0, packed.at[to], held.at[here.seq], here.worker(to, here.chan)).start()
 
+    def bring_late(step):
+        to = here.member(step)
+        remote(5, packed_late.at[to], held_late.at[here.seq], here.worker(to, here.chan)).start()
+
     def give(step):
         to = here.member(step)
         remote(1, done.at[to], returned.at[here.work_seq], (to, here.work_chan)).start()
+
+    def give_late(step):
+        to = here.member(step)
+        remote(6, done_late.at[to], returned_late.at[here.work_seq], (to, here.work_chan)).start()
 
     def scatter(step):
         to = towards(step)
@@ -203,7 +220,7 @@
         remote(2, cross_out.at[to], cross_in.at[here.work_chan], place).start()
 
     def spread(step):
-        to = (here.chan + 1 + step) % count
+        to = lax.rem(here.chan + 1 + step, count)
         remote(3, total.at[0], shares.at[here.work_seq], (here.work_chan, to)).start()
 
     origin = here.worker(here.seq, here.chan)
@@ -211,6 +228,7 @@
     taps_copy = remote(4, taps_hbm, taps_ref, origin)
     taps_copy.start()
     loop(blocks, bring)
+    loop(blocks, bring_late)
     for load in loads[6:]:
         load.wait()
     taps_copy.wait_recv()
@@ -230,11 +248,11 @@
     remote(0, packed, held, origin).wait_recv()
 
     arrived = held[...].astype(F32)
-    q, k, v, incoming, filt = (arrived[:, p * per : (p + 1) * per] for p in range(5))
-    query_conv = taps(q, weights[0], 1)
+    k, v, q, incoming = (arrived[:, p * per : (p + 1) * per] for p in range(4))
     key_conv = taps(k, weights[1], 1)
     value_conv = taps(v, weights[2], 1)
     gated = (key_conv * value_conv).reshape(blocks * per, slab)
+    query_conv = taps(q, weights[0], 1)
     conv_grad = (incoming * query_conv).reshape(blocks * per, slab)
 
     twist_re, twist_im = twist_re_ref[...], twist_im_ref[...]
@@ -262,33 +280,37 @@
         high = values.astype(BF16).astype(F32)
         return jnp.where(row < per // 2, high, values - high).astype(BF16)
 
-    high, low = split(jnp.concatenate([gated, conv_grad], axis=1))
-    both = triple(first_hi[...], first_lo[...], high, low)
-    g_re, g_im = finish(both[:bins, :slab], both[bins:, :slab])
-    c_re, c_im = finish(both[:bins, slab:], both[bins:, slab:])
-    cross = inverse(g_re * c_re + g_im * c_im, g_re * c_im - g_im * c_re)
-    cross = triple(last_hi[...], last_lo[...], *split(cross)).reshape(blocks, per, slab)
+    def ahead(values):
+        both = triple(first_hi[...], first_lo[...], *split(values))
+        return [
+            finish(both[:bins, at : at + slab], both[bins:, at : at + slab])
+            for at in range(0, values.shape[1], slab)
+        ]
+
+    def behind(values):
+        return triple(last_hi[...], last_lo[...], *split(values)).reshape(blocks, per, slab)
+
+    (g_re, g_im), (c_re, c_im) = ahead(jnp.concatenate([gated, conv_grad], axis=1))
+    cross = behind(inverse(g_re * c_re + g_im * c_im, g_re * c_im - g_im * c_re))
     cross_out[...] = halved(cross + pltpu.roll(cross, per // 2, 1))
-
-    own = (filt + pltpu.roll(filt, per // 2, 1)).reshape(blocks * per, slab)
-    own = triple(first_hi[...], first_lo[...], *split(own))
-    f_re, f_im = finish(own[:bins], own[bins:])
     loop(count - 1, scatter)
     kept = pltpu.make_async_copy(cross_out.at[here.work_chan], cross_in.at[here.work_chan], recv_sems.at[2])
     kept.start()
-    long = inverse(g_re * f_re - g_im * f_im, g_re * f_im + g_im * f_re)
-    back = inverse(f_re * c_re + f_im * c_im, f_re * c_im - f_im * c_re)
-    wide = triple(last_hi[...], last_lo[...], *split(jnp.concatenate([long, back], axis=1)))
-    long_conv = wide[:, :slab].reshape(blocks, per, slab)
-    gated_grad = wide[:, slab:].reshape(blocks, per, slab)
+
+    remote(5, packed_late, held_late, origin).wait_recv()
+    filt = held_late[...].astype(F32)
+    filt = (filt + pltpu.roll(filt, per // 2, 1)).reshape(blocks * per, slab)
+    ((f_re, f_im),) = ahead(filt)
+    long_conv = behind(inverse(g_re * f_re - g_im * f_im, g_re * f_im + g_im * f_re))
+    parts = [query_conv * long_conv, taps(incoming * long_conv, weights[0], -1)]
+    done[...] = jnp.concatenate(parts, axis=1).astype(BF16)
+    loop(blocks, give)
+    gated_grad = behind(inverse(f_re * c_re + f_im * c_im, f_re * c_im - f_im * c_re))
     parts = [
-        query_conv * long_conv,
-        taps(incoming * long_conv, weights[0], -1),
         taps(gated_grad * value_conv, weights[1], -1),
         taps(gated_grad * key_conv, weights[2], -1),
     ]
-    done[...] = jnp.concatenate(parts, axis=1).astype(BF16)
-    loop(blocks, give)
+    done_late[...] = jnp.concatenate(parts, axis=1).astype(BF16)
 
     remote(2, cross_out, cross_in, origin).wait_recv()
     summed = jnp.sum(cross_in[...].astype(F32), axis=0, keepdims=True)
@@ -297,23 +319,28 @@
 
     @pl.when(jnp.logical_not(alone))
     def _():
-        spread(count - 1)
-        remote(3, total.at[0], shares.at[0], origin).wait_send()
+        spread(jnp.int32(count - 1))
 
     @pl.when(alone)
     def _():
         pltpu.make_async_copy(total.at[0], shares.at[here.work_seq], recv_sems.at[3]).start()
 
+    loop(blocks, give_late)
     remote(1, done, returned, origin).wait_recv()
-    out_ref[...] = returned[...]
+    out_ref[:, : 2 * per] = returned[...]
+    remote(6, done_late, returned_late, origin).wait_recv()
+    out_ref[:, 2 * per :] = returned_late[...]
     remote(3, shares, shares, origin).wait_recv()
     share_ref[...] = shares[...]
     taps_copy.wait_send()
     remote(0, packed, held, origin).wait_send()
     remote(1, done, returned, origin).wait_send()
+    remote(5, packed_late, held_late, origin).wait_send()
+    remote(6, done_late, returned_late, origin).wait_send()
     fewer = pl.ds(0, count - 1)
     remote(2, cross_out.at[fewer], cross_in.at[fewer], origin).wait_send()
     remote(3, shares.at[fewer], shares.at[fewer], origin).wait_send()
+    pl.when(jnp.logical_not(alone))(lambda: remote(3, total.at[0], shares.at[0], origin).wait_send())
 
 
 def call(body, name, outs, *operands, space=pltpu.VMEM, **more):
@@ -346,11 +373,10 @@
         space=pl.ANY,
         scratch_shapes=[
             *[pltpu.VMEM(x.shape, x.dtype) for x in operands],
-            *[pltpu.VMEM((blocks, 5 * per, slab), BF16)] * 2,
-            *[pltpu.VMEM((blocks, 4 * per, slab), BF16)] * 2,
+            *[pltpu.VMEM((blocks, n * per, slab), BF16) for n in (4, 1, 4, 1, 2, 2, 2, 2)],
             small, small, pltpu.VMEM((1, per, slab), BF16), small,
             pltpu.SemaphoreType.DMA((len(operands) - 1,)),
-            *[pltpu.SemaphoreType.DMA((5,))] * 2,
+            *[pltpu.SemaphoreType.DMA((7,))] * 2,
         ],
         compiler_params=pltpu.CompilerParams(collective_id=0, has_side_effects=True),
     )

time: 74.5 us -> 74.5 us (level)
  no operation moved by 1% of the time
where the time goes in v2:
time: 74.5 us; the launch traced here: 74.3 us
  Pallas kernels  73.7 us (99%)
    pallas_call x2, Pallas kernels, call(): pl.pallas_call(body, name=name, out_shape=outs, in_specs=[pl.BlockSpec(me...  73.7 us

profile of v2, /device:TPU:1, one launch (start us, length us, event | category | flops | bytes accessed | tf_op | source)
XLA Modules:
  0.0 74.3 jit_solution(2772056779230222072)
XLA Ops:
  0.6 71.7 %whole.1 = (bf16[32,32,128]{2,1,0:T(8,128)(2,1)}, bf16[32,8,128]{2,1,0:T(8,128)(2,1)}) custom-call(bf16[128,256]{1,0:T(8,128)(2,1)} %q_hbm.1, bf16[128,256]{1,0:T(8,128)(2,1)} %k_hbm.1, bf16[128,256]{1,0:T(8,128)(2,1)} %v_hbm.1, f32[128,128]{1,0:T(8,128)} %f_hbm.1, bf16[128,256]{1,0:T(8,128)(2,1)} %ct_hbm.1, f32[3,3,256]{2,1,0:T(4,128)} %taps_hbm.1, ...), custom_call_target="tpu_custom_call" | custom-call | tf_op jit(solution)/shard_map/whole/pallas_call | solution.py:347
  72.4 2.0 %unpack.1 = (bf16[128,256]{1,0:T(8,128)(2,1)}, bf16[128,256]{1,0:T(8,128)(2,1)}, bf16[128,256]{1,0:T(8,128)(2,1)}, bf16[128,256]{1,0:T(8,128)(2,1)}, f32[128,128]{1,0:T(8,128)}) custom-call(bf16[32,32,128]{2,1,0:T(8,128)(2,1)} %get-tuple-element.7.in_ref, bf16[32,8,128]{2,1,0:T(8,128)(2,1)} %get-tuple-element.8.share_ref, ...), custom_call_target="tpu_custom_call" | custom-call | tf_op jit(solution)/shard_map/unpack/pallas_call | solution.py:347

commit v3 on v2

--- a/solution.py
+++ b/solution.py
@@ -153,7 +153,7 @@
     count = here.columns
     barrier = pltpu.get_barrier_semaphore()
     blocks, rows, slab = packed.shape
-    per = rows // 4
+    per = rows // 3
     alone = here.work_chan == here.seq
 
     def greet(pair):
@@ -162,11 +162,6 @@
     def towards(step):
         return lax.rem(here.work_chan + 1 + step, count)
 
-    def other(step):
-        return lax.rem(here.work_seq + 1 + step, blocks)
-
-    loop(blocks - 1, lambda step: greet(here.worker(other(step), here.seq)))
-    pl.when(jnp.logical_not(alone))(lambda: greet(here.worker(here.work_seq, here.seq)))
     loop(count - 1, lambda step: greet(here.worker(here.work_seq, towards(step))))
     loop(blocks, lambda step: greet((here.member(step), here.work_chan)))
 
@@ -189,8 +184,8 @@
         parts = [dot(pick, values, ((1,), (1,))).reshape(blocks, per, slab) for values in parts]
         return jnp.concatenate(parts, axis=1).astype(BF16)
 
-    packed[...] = pack(k_ref[...], v_ref[...], q_ref[...], ct_ref[...])
-    packed_late[...] = pack(jnp.concatenate([high, low], axis=1))
+    packed[...] = pack(k_ref[...], v_ref[...], jnp.concatenate([high, low], axis=1))
+    packed_late[...] = pack(q_ref[...], ct_ref[...])
 
     def remote(number, source, target, pair):
         return pltpu.make_async_remote_copy(
@@ -224,7 +219,7 @@
         remote(3, total.at[0], shares.at[here.work_seq], (here.work_chan, to)).start()
 
     origin = here.worker(here.seq, here.chan)
-    pl.semaphore_wait(barrier, blocks + count - 1 + blocks - jnp.where(alone, 1, 0))
+    pl.semaphore_wait(barrier, blocks + count - 1)
     taps_copy = remote(4, taps_hbm, taps_ref, origin)
     taps_copy.start()
     loop(blocks, bring)
@@ -248,12 +243,11 @@
     remote(0, packed, held, origin).wait_recv()
 
     arrived = held[...].astype(F32)
-    k, v, q, incoming = (arrived[:, p * per : (p + 1) * per] for p in range(4))
+    k, v, filt = (arrived[:, p * per : (p + 1) * per] for p in range(3))
     key_conv = taps(k, weights[1], 1)
     value_conv = taps(v, weights[2], 1)
     gated = (key_conv * value_conv).reshape(blocks * per, slab)
-    query_conv = taps(q, weights[0], 1)
-    conv_grad = (incoming * query_conv).reshape(blocks * per, slab)
+    filt = (filt + pltpu.roll(filt, per // 2, 1)).reshape(blocks * per, slab)
 
     twist_re, twist_im = twist_re_ref[...], twist_im_ref[...]
     bins = twist_re.shape[0]
@@ -290,20 +284,21 @@
     def behind(values):
         return triple(last_hi[...], last_lo[...], *split(values)).reshape(blocks, per, slab)
 
-    (g_re, g_im), (c_re, c_im) = ahead(jnp.concatenate([gated, conv_grad], axis=1))
+    (g_re, g_im), (f_re, f_im) = ahead(jnp.concatenate([gated, filt], axis=1))
+    long_conv = behind(inverse(g_re * f_re - g_im * f_im, g_re * f_im + g_im * f_re))
+
+    remote(5, packed_late, held_late, origin).wait_recv()
+    arrived = held_late[...].astype(F32)
+    q, incoming = arrived[:, :per], arrived[:, per:]
+    query_conv = taps(q, weights[0], 1)
+    ((c_re, c_im),) = ahead((incoming * query_conv).reshape(blocks * per, slab))
     cross = behind(inverse(g_re * c_re + g_im * c_im, g_re * c_im - g_im * c_re))
     cross_out[...] = halved(cross + pltpu.roll(cross, per // 2, 1))
+    parts = [query_conv * long_conv, taps(incoming * long_conv, weights[0], -1)]
+    done[...] = jnp.concatenate(parts, axis=1).astype(BF16)
     loop(count - 1, scatter)
     kept = pltpu.make_async_copy(cross_out.at[here.work_chan], cross_in.at[here.work_chan], recv_sems.at[2])
     kept.start()
-
-    remote(5, packed_late, held_late, origin).wait_recv()
-    filt = held_late[...].astype(F32)
-    filt = (filt + pltpu.roll(filt, per // 2, 1)).reshape(blocks * per, slab)
-    ((f_re, f_im),) = ahead(filt)
-    long_conv = behind(inverse(g_re * f_re - g_im * f_im, g_re * f_im + g_im * f_re))
-    parts = [query_conv * long_conv, taps(incoming * long_conv, weights[0], -1)]
-    done[...] = jnp.concatenate(parts, axis=1).astype(BF16)
     loop(blocks, give)
     gated_grad = behind(inverse(f_re * c_re + f_im * c_im, f_re * c_im - f_im * c_re))
     parts = [
@@ -311,6 +306,7 @@
         taps(gated_grad * key_conv, weights[2], -1),
     ]
     done_late[...] = jnp.concatenate(parts, axis=1).astype(BF16)
+    loop(blocks, give_late)
 
     remote(2, cross_out, cross_in, origin).wait_recv()
     summed = jnp.sum(cross_in[...].astype(F32), axis=0, keepdims=True)
@@ -320,12 +316,12 @@
     @pl.when(jnp.logical_not(alone))
     def _():
         spread(jnp.int32(count - 1))
+        remote(3, total.at[0], shares.at[0], origin).wait_send()
 
     @pl.when(alone)
     def _():
         pltpu.make_async_copy(total.at[0], shares.at[here.work_seq], recv_sems.at[3]).start()
 
-    loop(blocks, give_late)
     remote(1, done, returned, origin).wait_recv()
     out_ref[:, : 2 * per] = returned[...]
     remote(6, done_late, returned_late, origin).wait_recv()
@@ -340,7 +336,6 @@
     fewer = pl.ds(0, count - 1)
     remote(2, cross_out.at[fewer], cross_in.at[fewer], origin).wait_send()
     remote(3, shares.at[fewer], shares.at[fewer], origin).wait_send()
-    pl.when(jnp.logical_not(alone))(lambda: remote(3, total.at[0], shares.at[0], origin).wait_send())
 
 
 def call(body, name, outs, *operands, space=pltpu.VMEM, **more):
@@ -373,7 +368,7 @@
         space=pl.ANY,
         scratch_shapes=[
             *[pltpu.VMEM(x.shape, x.dtype) for x in operands],
-            *[pltpu.VMEM((blocks, n * per, slab), BF16) for n in (4, 1, 4, 1, 2, 2, 2, 2)],
+            *[pltpu.VMEM((blocks, n * per, slab), BF16) for n in (3, 2, 3, 2, 2, 2, 2, 2)],
             small, small, pltpu.VMEM((1, per, slab), BF16), small,
             pltpu.SemaphoreType.DMA((len(operands) - 1,)),
             *[pltpu.SemaphoreType.DMA((7,))] * 2,

time: 74.5 us -> 72.4 us (0.972)
  Pallas kernels: 73.7 us -> 71.3 us
    pallas_call x2, Pallas kernels: 73.7 us -> 71.3 us  [call(): pl.pallas_call(body, name=name, out_shape=outs, in_specs=[pl.BlockSpec(me...]
where the time goes in v3:
time: 72.4 us; the launch traced here: 71.9 us
  Pallas kernels  71.3 us (98%)
    pallas_call x2, Pallas kernels, call(): pl.pallas_call(body, name=name, out_shape=outs, in_specs=[pl.BlockSpec(me...  71.3 us

profile of v3, /device:TPU:1, one launch (start us, length us, event | category | flops | bytes accessed | tf_op | source)
XLA Modules:
  0.0 71.9 jit_solution(15004234342464467201)
XLA Ops:
  0.6 69.3 %whole.1 = (bf16[32,32,128]{2,1,0:T(8,128)(2,1)}, bf16[32,8,128]{2,1,0:T(8,128)(2,1)}) custom-call(bf16[128,256]{1,0:T(8,128)(2,1)} %q_hbm.1, bf16[128,256]{1,0:T(8,128)(2,1)} %k_hbm.1, bf16[128,256]{1,0:T(8,128)(2,1)} %v_hbm.1, f32[128,128]{1,0:T(8,128)} %f_hbm.1, bf16[128,256]{1,0:T(8,128)(2,1)} %ct_hbm.1, f32[3,3,256]{2,1,0:T(4,128)} %taps_hbm.1, ...), custom_call_target="tpu_custom_call" | custom-call | tf_op jit(solution)/shard_map/whole/pallas_call | solution.py:342
  69.9 2.0 %unpack.1 = (bf16[128,256]{1,0:T(8,128)(2,1)}, bf16[128,256]{1,0:T(8,128)(2,1)}, bf16[128,256]{1,0:T(8,128)(2,1)}, bf16[128,256]{1,0:T(8,128)(2,1)}, f32[128,128]{1,0:T(8,128)}) custom-call(bf16[32,32,128]{2,1,0:T(8,128)(2,1)} %get-tuple-element.7.in_ref, bf16[32,8,128]{2,1,0:T(8,128)(2,1)} %get-tuple-element.8.share_ref, ...), custom_call_target="tpu_custom_call" | custom-call | tf_op jit(solution)/shard_map/unpack/pallas_call | solution.py:342

commit v4 on v3

--- a/solution.py
+++ b/solution.py
@@ -116,6 +116,13 @@
     def worker(self, seq, chan):
         return self.moved(seq, chan, self.run // 2)
 
+    def block(self, chan):
+        half = self.run // 2
+        column = lax.rem(chan, self.run)
+        far = lax.rem(lax.rem(lax.div(self.work_seq, 2), 2) + lax.div(column, half), 2)
+        order = lax.div(chan, self.run) * half + lax.rem(column, half)
+        return lax.div(order, 2) * 4 + far * 2 + lax.rem(order, 2)
+
     def member(self, step):
         rows = self.blocks // 4
         row = lax.rem(lax.div(self.seq, 4) + lax.div(step, 4) + rows // 2, rows)
@@ -154,7 +161,8 @@
     barrier = pltpu.get_barrier_semaphore()
     blocks, rows, slab = packed.shape
     per = rows // 3
-    alone = here.work_chan == here.seq
+    target = here.block(here.work_chan)
+    alone = target == here.seq
 
     def greet(pair):
         pl.semaphore_signal(barrier, inc=1, **device(pair))
@@ -212,11 +220,11 @@
     def scatter(step):
         to = towards(step)
         place = here.worker(here.work_seq, to)
-        remote(2, cross_out.at[to], cross_in.at[here.work_chan], place).start()
+        remote(2, cross_out.at[here.block(to)], cross_in.at[here.work_chan], place).start()
 
     def spread(step):
         to = lax.rem(here.chan + 1 + step, count)
-        remote(3, total.at[0], shares.at[here.work_seq], (here.work_chan, to)).start()
+        remote(3, total.at[0], shares.at[here.work_seq], (target, to)).start()
 
     origin = here.worker(here.seq, here.chan)
     pl.semaphore_wait(barrier, blocks + count - 1)
@@ -294,11 +302,11 @@
     ((c_re, c_im),) = ahead((incoming * query_conv).reshape(blocks * per, slab))
     cross = behind(inverse(g_re * c_re + g_im * c_im, g_re * c_im - g_im * c_re))
     cross_out[...] = halved(cross + pltpu.roll(cross, per // 2, 1))
+    loop(count - 1, scatter)
+    kept = pltpu.make_async_copy(cross_out.at[target], cross_in.at[here.work_chan], recv_sems.at[2])
+    kept.start()
     parts = [query_conv * long_conv, taps(incoming * long_conv, weights[0], -1)]
     done[...] = jnp.concatenate(parts, axis=1).astype(BF16)
-    loop(count - 1, scatter)
-    kept = pltpu.make_async_copy(cross_out.at[here.work_chan], cross_in.at[here.work_chan], recv_sems.at[2])
-    kept.start()
     loop(blocks, give)
     gated_grad = behind(inverse(f_re * c_re + f_im * c_im, f_re * c_im - f_im * c_re))
     parts = [
@@ -323,11 +331,14 @@
         pltpu.make_async_copy(total.at[0], shares.at[here.work_seq], recv_sems.at[3]).start()
 
     remote(1, done, returned, origin).wait_recv()
-    out_ref[:, : 2 * per] = returned[...]
+    first_out = pltpu.make_async_copy(returned, out_ref.at[:, : 2 * per], load_sems.at[0])
+    first_out.start()
     remote(6, done_late, returned_late, origin).wait_recv()
-    out_ref[:, 2 * per :] = returned_late[...]
+    second_out = pltpu.make_async_copy(returned_late, out_ref.at[:, 2 * per :], load_sems.at[1])
+    second_out.start()
     remote(3, shares, shares, origin).wait_recv()
-    share_ref[...] = shares[...]
+    share_out = pltpu.make_async_copy(shares, share_ref, load_sems.at[2])
+    share_out.start()
     taps_copy.wait_send()
     remote(0, packed, held, origin).wait_send()
     remote(1, done, returned, origin).wait_send()
@@ -336,15 +347,17 @@
     fewer = pl.ds(0, count - 1)
     remote(2, cross_out.at[fewer], cross_in.at[fewer], origin).wait_send()
     remote(3, shares.at[fewer], shares.at[fewer], origin).wait_send()
-
-
-def call(body, name, outs, *operands, space=pltpu.VMEM, **more):
+    for leaving in (first_out, second_out, share_out):
+        leaving.wait()
+
+
+def call(body, name, outs, *operands, space=pltpu.VMEM, out_space=pltpu.VMEM, **more):
     return pl.pallas_call(
         body,
         name=name,
         out_shape=outs,
         in_specs=[pl.BlockSpec(memory_space=space)] * len(operands),
-        out_specs=jax.tree.map(lambda _: pl.BlockSpec(memory_space=pltpu.VMEM), outs),
+        out_specs=jax.tree.map(lambda _: pl.BlockSpec(memory_space=out_space), outs),
         **more,
     )(*operands)
 
@@ -366,6 +379,7 @@
         [shape((blocks, 4 * per, slab)), shape((blocks, per, slab))],
         *operands,
         space=pl.ANY,
+        out_space=pl.ANY,
         scratch_shapes=[
             *[pltpu.VMEM(x.shape, x.dtype) for x in operands],
             *[pltpu.VMEM((blocks, n * per, slab), BF16) for n in (3, 2, 3, 2, 2, 2, 2, 2)],

time: 72.4 us -> 72.9 us (level)
  Pallas kernels: 71.3 us -> 72.1 us
    pallas_call x2, Pallas kernels: 71.3 us -> 72.1 us  [call(): pl.pallas_call(body, name=name, out_shape=outs, in_specs=[pl.BlockSpec(me...]
where the time goes in v4:
time: 72.9 us; the launch traced here: 72.7 us
  Pallas kernels  72.1 us (99%)
    pallas_call x2, Pallas kernels, call(): pl.pallas_call(body, name=name, out_shape=outs, in_specs=[pl.BlockSpec(me...  72.1 us

profile of v4, /device:TPU:1, one launch (start us, length us, event | category | flops | bytes accessed | tf_op | source)
XLA Modules:
  0.0 72.7 jit_solution(8777510089123320249)
XLA Ops:
  0.6 70.1 %whole.1 = (bf16[32,32,128]{2,1,0:T(8,128)(2,1)}, bf16[32,8,128]{2,1,0:T(8,128)(2,1)}) custom-call(bf16[128,256]{1,0:T(8,128)(2,1)} %q_hbm.1, bf16[128,256]{1,0:T(8,128)(2,1)} %k_hbm.1, bf16[128,256]{1,0:T(8,128)(2,1)} %v_hbm.1, f32[128,128]{1,0:T(8,128)} %f_hbm.1, bf16[128,256]{1,0:T(8,128)(2,1)} %ct_hbm.1, f32[3,3,256]{2,1,0:T(4,128)} %taps_hbm.1, ...), custom_call_target="tpu_custom_call" | custom-call | tf_op jit(solution)/shard_map/whole/pallas_call | solution.py:355
  70.7 2.0 %unpack.1 = (bf16[128,256]{1,0:T(8,128)(2,1)}, bf16[128,256]{1,0:T(8,128)(2,1)}, bf16[128,256]{1,0:T(8,128)(2,1)}, bf16[128,256]{1,0:T(8,128)(2,1)}, f32[128,128]{1,0:T(8,128)}) custom-call(bf16[32,32,128]{2,1,0:T(8,128)(2,1)} %get-tuple-element.7.in_ref, bf16[32,8,128]{2,1,0:T(8,128)(2,1)} %get-tuple-element.8.share_ref, ...), custom_call_target="tpu_custom_call" | custom-call | tf_op jit(solution)/shard_map/unpack/pallas_call | solution.py:355
